TPU v7x, 512 devices: a whole 4x8x8 slice. The times are simulated.
512 devices in a mesh: beam: 32 (over y, x), trans: 16 (over z, core).
Axes of the slice: x: 4, y: 8, z: 8, core: 2. Of those that a mesh axis runs over, the one named last changes fastest.
Arguments:
- field_in: float32 [2, 128, 256, 256], P(None, 'beam', 'trans'), may hold values from -4 to 4
- phases: float32 [128, 4096], P('beam'), may hold values from -3.140625 to 3.140625
- energy: float32 [128, 4096], P('beam'), may hold values from -3 to 3
- row_cell: int32 [128, 4096], P('beam'), may hold values from 32 to 223
- col_cell: int32 [128, 4096], P('beam'), may hold values from 32 to 223
- weight: int32 [128, 4096], P('beam'), may hold values from 1 to 15
- charge: int32 [128], P('beam'), may hold values from 256 to 1024
- pole_rate: float32 [8], replicated, may hold values from 0.001953125 to 0.5
- pole_freq: float32 [8], replicated, may hold values from 0 to 0.3
- pole_amp: float32 [8], replicated, may hold values from -3 to 3
Outputs:
- field_out: float32 [2, 128, 256, 256], P(None, 'beam', 'trans')
- phase_out: float32 [128, 4096], P('beam')
- energy_out: float32 [128, 4096], P('beam')
All inputs are finite; a program needn't handle non-finite values.
Results may differ from a plain program's by a relative error of at most 0.00042.
Values sent between devices are 32-bit elements; how exact they have to be, the bound alone decides.
No kernel may reach another device: no remote copies, remote signals or barrier semaphores. Data moves between devices by JAX's collectives and lax.ppermute only.
A program may use at most 64 MiB of HBM per device.

v0:
```python
import functools

import jax
import jax.numpy as jnp
import numpy as np
from jax import lax
from jax.experimental import pallas as pl
from jax.experimental.pallas import tpu as pltpu
from jax.sharding import PartitionSpec as P

diffraction = 20.0
kick_gain = 0.5
deposit_gain = 0.05
wake_gain = 3.0
charge_unit = 1024.0

GRID = 256
SLICES = 128
NPART = 4096
BEAM = 32
TRANS = 16
LOW, HIGH = 32, 224
SPAN = HIGH - LOW
TABLE = (2, 2 * GRID, GRID)
ROWS, WIDE = 8, 512
JOINT = ("beam", "trans")
QUADS = [[4 * r + c for c in range(4)] for r in range(4)]

f32 = jnp.float32
bf16 = jnp.bfloat16


def propagation_table():
    n = np.arange(GRID)
    centred = ((n + GRID // 2) % GRID - GRID // 2) / GRID
    k = np.exp(-1j * diffraction * centred**2)
    h = np.fft.ifft(k)
    a = h[(n[:, None] - n[None, :]) % GRID]
    parts = np.stack([a.real, a.imag]).astype(np.float32)
    high = parts.astype(jnp.bfloat16)
    low = (parts - high.astype(np.float32)).astype(jnp.bfloat16)
    return np.stack([part.reshape(2 * GRID, GRID) for part in (high, low)])


def moved(fn):
    out = []
    for b in range(BEAM):
        for t in range(TRANS):
            b2, t2 = fn(b, t)
            out.append((b * TRANS + t, (b2 % BEAM) * TRANS + t2))
    return out


TO_PREVIOUS = moved(lambda b, t: ((4 * b + t % 4 - 1) // 4, t // 4 * 4 + (t % 4 - 1) % 4))
NEXT_BEAM = [(b, (b + 1) % BEAM) for b in range(BEAM)]


def split(x):
    high = x.astype(bf16)
    return high, (x - high.astype(f32)).astype(bf16)


def dot(a, b):
    return jnp.dot(a, b, preferred_element_type=f32)


def times_right(xr, xi, high, low):
    p = []
    for x in (xr, xi):
        xh, xl = split(x)
        for k in range(2):
            h, w = high[k * GRID : (k + 1) * GRID], low[k * GRID : (k + 1) * GRID]
            p.append(dot(xh, h) + dot(xl, h) + dot(xh, w))
    return p[0] - p[3], p[1] + p[2]


def times_left(ah, al, xr, xi):
    m = ah.shape[0] // 2
    xh, xl = split(jnp.concatenate([xr, xi], axis=1))
    q = []
    for k in range(2):
        high, low = ah[k * m : (k + 1) * m], al[k * m : (k + 1) * m]
        q.append(dot(high, xh) + dot(low, xh) + dot(high, xl))
    return q[0][:, :GRID] - q[1][:, GRID:], q[1][:, :GRID] + q[0][:, GRID:]


def iota_rows(first, count):
    return lax.broadcasted_iota(jnp.int32, (count, WIDE), 0).astype(f32) + float(first)


def hot(values, rows_bf):
    return jnp.where(rows_bf == values.astype(bf16), jnp.ones((), bf16), jnp.zeros((), bf16))


def probe(fr, fi, rows, cols, out_re, out_im):
    high, low = split(jnp.concatenate([fr[LOW:HIGH], fi[LOW:HIGH]], axis=0))
    col_iota = iota_rows(0, GRID).astype(bf16)
    offset = rows.astype(jnp.int32) - LOW
    inside = lax.broadcasted_iota(jnp.int32, (8, WIDE), 0)
    for q in range(ROWS):
        col_hot = hot(cols[q : q + 1], col_iota)
        found = dot(high, col_hot) + dot(low, col_hot)
        at = jnp.broadcast_to(offset[q : q + 1], (8, WIDE))
        group = at >> 3
        got_re, got_im = found[:8], found[SPAN : SPAN + 8]
        for k in range(1, SPAN // 8):
            here = group == k
            got_re = jnp.where(here, found[8 * k : 8 * k + 8], got_re)
            got_im = jnp.where(here, found[SPAN + 8 * k : SPAN + 8 * k + 8], got_im)
        mine = (at & 7) == inside
        out_re[q : q + 1, :] = jnp.sum(jnp.where(mine, got_re, 0.0), axis=0, keepdims=True)
        out_im[q : q + 1, :] = jnp.sum(jnp.where(mine, got_im, 0.0), axis=0, keepdims=True)


def deposit(angles, weights, rows, cols):
    v = (weights * jnp.cos(angles)).astype(bf16)
    u = (-weights * jnp.sin(angles)).astype(bf16)
    col_iota = iota_rows(0, GRID).astype(bf16)
    row_iota = iota_rows(LOW, SPAN).astype(bf16)
    zero = jnp.zeros((), bf16)
    total = [jnp.zeros((SPAN, GRID), f32)] * 2
    for q in range(ROWS):
        col_hot = hot(cols[q : q + 1], col_iota)
        mask = row_iota == rows[q : q + 1].astype(bf16)
        for k, value in enumerate((v, u)):
            left = jnp.where(mask, value[q : q + 1], zero)
            total[k] = total[k] + lax.dot_general(
                left, col_hot, (((1,), (1,)), ((), ())), preferred_element_type=f32
            )
    return total


def deposited(field, change, strength):
    return jnp.concatenate(
        [field[:LOW], field[LOW:HIGH] + strength * change, field[HIGH:]], axis=0
    )


def place():
    t = lax.axis_index("trans")
    return lax.axis_index("beam"), t, t % 4, t // 4


def prep_body(field, phases, energy, row, col, weight, charge, send, own, charges):
    b, _, c, _ = place()
    for part in range(2):
        for k in range(2):
            send[part * 2 + k] = field[part, 2 + k]
    own_one, own_two = jnp.maximum(c - 2, 0), jnp.maximum(c - 1, 0)

    def pick(ref, index, slot):
        line = ref[pl.ds(index, 1), :].astype(f32)
        for q in range(ROWS):
            own[slot, q : q + 1, :] = line[:, q * WIDE : (q + 1) * WIDE]

    for slot, ref in enumerate((phases, energy, row, col, weight)):
        pick(ref, own_one, slot)
        for k in range(2):
            line = ref[2 + k : 3 + k, :].astype(f32)
            for q in range(ROWS):
                for half in range(2):
                    begin = q * WIDE + half * 256
                    at = half * 8 + q
                    send[4 + 2 * slot + k, at : at + 1, :] = line[:, begin : begin + 256]
    for slot, ref in enumerate((row, col, weight)):
        pick(ref, own_two, 5 + slot)
    lane = lax.broadcasted_iota(jnp.int32, (1, SLICES), 1)
    line = jnp.zeros((1, SLICES), f32)
    for k in range(4):
        line = jnp.where(lane == 4 * b + k, charge[k].astype(f32) / charge_unit, line)
    charges[...] = line


def pack_body(field, received, out):
    for c in range(4):
        for part in range(2):
            piece = received[part * 2 + c] if c < 2 else field[part, c - 2]
            for half in range(2):
                at = (part * 2 + half) * 16
                for r in range(4):
                    out[4 * r + c, at : at + 16, :] = piece[:, half * 128 : (half + 1) * 128]


def whole_field(x, part):
    halves = [
        x[:, (part * 2 + half) * 16 : (part * 2 + half + 1) * 16, :].reshape(GRID, 128)
        for half in range(2)
    ]
    return jnp.concatenate(halves, axis=1)


def period_one(own, received, c, slot):
    piece = received[4 + 2 * slot + jnp.minimum(c, 1)]
    piece = jnp.concatenate([piece[:8], piece[8:]], axis=1)
    return jnp.where(c < 2, piece, own[slot])


def period_two(own, received, c, slot):
    piece = received[4 + 2 * slot + 1]
    piece = jnp.concatenate([piece[:8], piece[8:]], axis=1)
    return jnp.where(c < 1, piece, own[slot + 3])


def wake_sums(g, charges, rate, freq, amp, extra):
    source = lax.broadcasted_iota(jnp.int32, (8, 128), 1)
    pole = lax.broadcasted_iota(jnp.int32, (8, 128), 0)
    rates, freqs, amps = (jnp.zeros((8, 128), f32) for _ in range(3))
    for k in range(8):
        rates = jnp.where(pole == k, rate[k], rates)
        freqs = jnp.where(pole == k, freq[k], freqs)
        amps = jnp.where(pole == k, amp[k], amps)

    def total(value):
        return jnp.sum(jnp.sum(value, axis=0, keepdims=True), axis=1, keepdims=True)

    for k, back in enumerate((2, 1)):
        s = (g + SLICES - back) % SLICES
        steps = jnp.maximum(s - source, 0).astype(f32)
        power = jnp.exp(-rates * steps) * jnp.cos(freqs * steps)
        reach = jnp.where(source < s, power, jnp.where(source == s, 0.5, 0.0))
        wake = wake_gain / SLICES * total(amps * reach * charges)
        norm = total(jnp.where((source == s) & (pole == 0), charges, 0.0))
        extra[k] = jnp.broadcast_to(wake, (8, 128))
        extra[2 + k] = jnp.broadcast_to(norm, (8, 128))


def first_body(x, own, received, charges, rate, freq, amp, states, extra, re, im):
    b, _, c, _ = place()
    wake_sums(4 * b + c, charges[...], rate, freq, amp, extra)
    take = functools.partial(period_one, own, received, c)
    fr, fi = whole_field(x, 0), whole_field(x, 1)
    probe(fr, fi, take(2), take(3), re, im)
    angles = take(0)
    energies = (
        take(1)
        - kick_gain * (re[...] * jnp.cos(angles) - im[...] * jnp.sin(angles))
        - extra[0, 0:1, 0:1]
    )
    states[0] = angles + energies
    states[1] = energies


def second_body(x, states, own, received, extra, tall, field, re, im, again):
    again[...] = tall[...]
    b, _, c, _ = place()
    take = functools.partial(period_one, own, received, c)
    br, bi = deposit(states[0], take(4), take(2), take(3))
    strength = deposit_gain * extra[2, 0:1, 0:1]
    fr = deposited(whole_field(x, 0), br, strength)
    fi = deposited(whole_field(x, 1), bi, strength)
    fr, fi = times_right(fr, fi, tall[0], tall[1])
    fr, fi = times_left(tall[0], tall[1], fr, fi)
    first = (b == 0) & (c == 1)
    fr = jnp.where(first, 0.0, fr)
    fi = jnp.where(first, 0.0, fi)
    field[0] = fr
    field[1] = fi
    take = functools.partial(period_two, own, received, c)
    probe(fr, fi, take(2), take(3), re, im)


def third_body(states, extra, re, im, out):
    angles = states[0]
    energies = (
        states[1]
        - kick_gain * (re[...] * jnp.cos(angles) - im[...] * jnp.sin(angles))
        - extra[1, 0:1, 0:1]
    )
    out[0] = angles + energies
    out[1] = energies


def fourth_body(field, states, own, received, extra, tall, out):
    b, _, c, r = place()
    take = functools.partial(period_two, own, received, c)
    br, bi = deposit(states[0], take(4), take(2), take(3))
    strength = deposit_gain * extra[3, 0:1, 0:1]
    fr = deposited(field[0], br, strength)
    fi = deposited(field[1], bi, strength)
    at = pl.multiple_of(r * 64, 64)
    ah, al = (
        jnp.concatenate([tall[k, pl.ds(at, 64), :], tall[k, pl.ds(GRID + at, 64), :]], axis=0)
        for k in range(2)
    )
    fr, fi = times_left(ah, al, fr, fi)
    fr, fi = times_right(fr, fi, tall[0], tall[1])
    empty = (b == 0) & (c == 0)
    for part, value in enumerate((fr, fi)):
        value = jnp.where(empty, 0.0, value)
        for j in range(4):
            out[j, part * 16 : part * 16 + 16, :] = value[16 * j : 16 * j + 16]


def last_body(x, field, phase, energy):
    for c in range(4):
        for part in range(2):
            field[part, c] = x[c, part * 16 : part * 16 + 16, :]
        for k, target in enumerate((phase, energy)):
            for half in range(2):
                at = 32 + (k * 2 + half) * 8
                piece = x[c, at : at + 8, :]
                for q in range(ROWS):
                    begin = q * WIDE + half * 256
                    target[c : c + 1, begin : begin + 256] = piece[q : q + 1]


def call(body, outs, *args, scalars=(), plain=(), last=False, room=0):
    specs, inputs = [], []
    for k, arg in enumerate(args):
        specs.append(pl.BlockSpec(memory_space=pltpu.SMEM if k in scalars else pltpu.VMEM))
        if k not in scalars and k not in plain:
            arg = pltpu.with_memory_space_constraint(arg, pltpu.VMEM)
        inputs.append(arg)
    kind = jax.ShapeDtypeStruct if last else pltpu.VMEM
    return pl.pallas_call(
        body,
        out_shape=[kind(shape, bf16 if shape == TABLE else f32) for shape in outs],
        in_specs=specs,
        out_specs=[pl.BlockSpec(memory_space=pltpu.VMEM) for _ in outs],
        compiler_params=pltpu.CompilerParams(vmem_limit_bytes=room << 20) if room else None,
    )(*inputs)


def shards(
    field_in, phases, energy, row_cell, col_cell, weight, charge, pole_rate, pole_freq, pole_amp
):
    tall = jnp.asarray(propagation_table())
    kept = (8, ROWS, WIDE)
    state_shape = (2, ROWS, WIDE)
    line = (ROWS, WIDE)
    send, own, charges = call(
        prep_body,
        [(14, 16, GRID), kept, (1, SLICES)],
        field_in, phases, energy, row_cell, col_cell, weight, charge,
        scalars=(6,), plain=range(6),
    )
    received = lax.ppermute(send, "beam", NEXT_BEAM)
    charges = jnp.broadcast_to(charges[None], (BEAM, 1, SLICES))
    charges = lax.all_to_all(charges, "beam", 0, 0, tiled=True)
    charges = jnp.sum(charges, axis=0)
    (packed,) = call(pack_body, [(TRANS, 64, 128)], field_in, received)
    x = lax.all_to_all(packed, "trans", 0, 0, tiled=True)
    states, extra, _, _ = call(
        first_body,
        [state_shape, (4, 8, 128), line, line],
        x, own, received, charges, pole_rate, pole_freq, pole_amp,
        scalars=(4, 5, 6),
    )
    following = lax.ppermute(states, JOINT, TO_PREVIOUS)
    field, re, im, tall = call(
        second_body,
        [(2, GRID, GRID), line, line, TABLE],
        x, states, own, received, extra, tall, room=24,
    )
    (final,) = call(third_body, [state_shape], following, extra, re, im, room=24)
    home = lax.ppermute(final, JOINT, TO_PREVIOUS)
    (bands,) = call(
        fourth_body, [(4, 32, GRID)], field, final, own, received, extra, tall, room=24
    )
    home = jnp.concatenate([home[..., :256], home[..., 256:]], axis=1).reshape(32, 256)
    both = jnp.concatenate([bands, jnp.broadcast_to(home[None], (4, 32, 256))], axis=1)
    y = lax.all_to_all(both, "trans", 0, 0, tiled=True, axis_index_groups=QUADS)
    return tuple(
        call(last_body, [(2, 4, 16, GRID), (4, NPART), (4, NPART)], y, last=True)
    )


def solution(mesh):
    placed = (
        P(None, "beam", "trans", None),
        P("beam", None),
        P("beam", None),
        P("beam", None),
        P("beam", None),
        P("beam", None),
        P("beam"),
        P(),
        P(),
        P(),
    )
    return jax.shard_map(
        shards,
        mesh=mesh,
        in_specs=placed,
        out_specs=(P(None, "beam", "trans", None), P("beam", None), P("beam", None)),
        check_vma=False,
    )
```

profile of v0, /device:TPU:1, one launch (start us, length us, event | category | flops | bytes accessed | tf_op | source)
XLA Modules:
  0.0 79.0 jit_solution(16697158795275100637)
XLA Ops:
  0.6 0.0 copy-start
  0.6 1.2 %shard_map.130 = (f32[14,16,256]{2,1,0:T(8,128)S(1)}, f32[8,8,512]{2,1,0:T(8,128)S(1)}, f32[1,128]{1,0:T(1,128)S(1)}) custom-call(f32[2,4,16,256]{3,2,1,0:T(8,128)} %field.3, f32[4,4096]{1,0:T(4,128)} %phases.1, f32[4,4096]{1,0:T(4,128)} %energy.1, s32[4,4096]{1,0:T(4,128)} %row.1, s32[4,4096]{1,0:T(4,128)} %col.1, s32[4,4096]{1,0:T(4,128)} %weight.1, s32[4]{0:T(128)} %charge.1), custom_call_target="tpu_custom_call" | custom-call | tf_op jit(solution)/shard_map/pallas_call | solution.py:315
  1.8 3.9 %collective-permute-start = (f32[14,16,256]{2,1,0:T(8,128)S(1)}, f32[14,16,256]{2,1,0:T(8,128)S(1)}, u32[]{:S(2)}, u32[]{:S(2)}) collective-permute-start(f32[14,16,256]{2,1,0:T(8,128)S(1)} %get-tuple-element.12), channel_id=1, source_target_pairs={{0,16},{16,32},{32,48},{48,64},{64,80},{80,96},{96,112},{112,128},... | collective-permute-start | bytes 688136 | tf_op jit(solution)/shard_map/ppermute | solution.py:337
  5.8 0.6 broadcast_in_dim.16
  6.4 9.4 %all-to-all-start.1 = ((f32[32,1,128]{2,1,0:T(1,128)}), f32[32,1,128]{2,1,0:T(1,128)S(1)}, u32[]{:S(2)}, u32[]{:S(2)}) async-start(f32[32,1,128]{2,1,0:T(1,128)} %broadcast_in_dim.16), calls=%async_computation.1 | async-start | bytes 32768 | tf_op jit(solution)/shard_map/all_to_all | solution.py:339
  15.8 0.0 collective-permute-done.received
  15.8 0.0 copy-done
  15.8 0.8 %shard_map.131 = f32[16,64,128]{2,1,0:T(8,128)} custom-call(f32[2,4,16,256]{3,2,1,0:T(8,128)S(1)} %copy-done, f32[14,16,256]{2,1,0:T(8,128)S(1)} %collective-permute-done.received), custom_call_target="tpu_custom_call" | custom-call | tf_op jit(solution)/shard_map/pallas_call | solution.py:315
  16.6 7.7 %all-to-all-done.1 = f32[32,1,128]{2,1,0:T(1,128)S(1)} async-done(((f32[32,1,128]{2,1,0:T(1,128)}), f32[32,1,128]{2,1,0:T(1,128)S(1)}, u32[]{:S(2)}, u32[]{:S(2)}) %all-to-all-start.1) | async-done | bytes 16416 | tf_op jit(solution)/shard_map/all_to_all | solution.py:339
  24.3 12.7 %all-to-all-start = ((f32[16,64,128]{2,1,0:T(8,128)}), f32[16,64,128]{2,1,0:T(8,128)S(1)}, u32[]{:S(2)}, u32[]{:S(2)}) async-start(f32[16,64,128]{2,1,0:T(8,128)} %shard_map.131), calls=%async_computation | async-start | bytes 1048576 | tf_op jit(solution)/shard_map/all_to_all | solution.py:342
  37.0 0.0 copy-start.1
  37.0 17.2 %all-to-all-done.x = f32[16,64,128]{2,1,0:T(8,128)S(1)} async-done(((f32[16,64,128]{2,1,0:T(8,128)}), f32[16,64,128]{2,1,0:T(8,128)S(1)}, u32[]{:S(2)}, u32[]{:S(2)}) %all-to-all-start) | async-done | bytes 524320 | tf_op jit(solution)/shard_map/all_to_all | solution.py:342
  54.2 3.1 %shard_map.132 = (f32[2,8,512]{2,1,0:T(8,128)S(1)}, f32[4,8,128]{2,1,0:T(8,128)S(1)}, f32[8,512]{1,0:T(8,128)}, f32[8,512]{1,0:T(8,128)}) custom-call(f32[16,64,128]{2,1,0:T(8,128)S(1)} %all-to-all-done.x, f32[8,8,512]{2,1,0:T(8,128)S(1)} %get-tuple-element.13.own, f32[14,16,256]{2,1,0:T(8,128)S(1)} %collective-permute-done.received, f32[1,128]{1,0:T(1,128)S(1)} %bitcast.4, ...), custom_call_target="tpu_custom_call" | custom-call | tf_op jit(solution)/shard_map/pallas_call | solution.py:315
  57.4 1.9 %collective-permute-start.1 = (f32[2,8,512]{2,1,0:T(8,128)S(1)}, f32[2,8,512]{2,1,0:T(8,128)S(1)}, u32[]{:S(2)}, u32[]{:S(2)}) collective-permute-start(f32[2,8,512]{2,1,0:T(8,128)S(1)} %get-tuple-element.15.states), channel_id=1, source_target_pairs={{0,499},{1,0},{2,1},{3,2},{4,503},{5,4},{6,5},{7,6},{8,507},{9,8},... | collective-permute-start | bytes 98312 | tf_op jit(solution)/shard_map/ppermute | solution.py:349
  59.3 0.0 copy-done.1
  59.3 4.3 %shard_map.133 = (f32[2,256,256]{2,1,0:T(8,128)S(1)}, f32[8,512]{1,0:T(8,128)S(1)}, f32[8,512]{1,0:T(8,128)S(1)}, bf16[2,512,256]{2,1,0:T(8,128)(2,1)S(1)}) custom-call(f32[16,64,128]{2,1,0:T(8,128)S(1)} %all-to-all-done.x, f32[2,8,512]{2,1,0:T(8,128)S(1)} %get-tuple-element.15.states, f32[8,8,512]{2,1,0:T(8,128)S(1)} %get-tuple-element.13.own, ...), custom_call_target="tpu_custom_call" | custom-call | tf_op jit(solution)/shard_map/pallas_call | solution.py:315
  63.6 0.0 collective-permute-done.1.states
  63.6 0.1 shard_map.134.states
  63.7 1.9 %collective-permute-start.2 = (f32[2,8,512]{2,1,0:T(8,128)S(1)}, f32[2,8,512]{2,1,0:T(8,128)S(1)}, u32[]{:S(2)}, u32[]{:S(2)}) collective-permute-start(f32[2,8,512]{2,1,0:T(8,128)S(1)} %shard_map.134.states), channel_id=1, source_target_pairs={{0,499},{1,0},{2,1},{3,2},{4,503},{5,4},{6,5},{7,6},{8,507},{9,8},... | collective-permute-start | bytes 98312 | tf_op jit(solution)/shard_map/ppermute | solution.py:356
  65.6 2.2 %shard_map.135 = f32[4,32,256]{2,1,0:T(8,128)S(1)} custom-call(f32[2,256,256]{2,1,0:T(8,128)S(1)} %get-tuple-element.17.field, f32[2,8,512]{2,1,0:T(8,128)S(1)} %shard_map.134.states, f32[8,8,512]{2,1,0:T(8,128)S(1)} %get-tuple-element.13.own, f32[14,16,256]{2,1,0:T(8,128)S(1)} %collective-permute-done.received, f32[4,8,128]{2,1,0:T(8,128)S(1)} %get-tuple-element.16.extra, ...), custom_call_target="tpu_custom_call" | custom-call | tf_op jit(solution)/shard_map/pallas_call | solution.py:315
  67.9 1.1 %collective-permute-done.2 = f32[2,8,512]{2,1,0:T(8,128)S(1)} collective-permute-done((f32[2,8,512]{2,1,0:T(8,128)S(1)}, f32[2,8,512]{2,1,0:T(8,128)S(1)}, u32[]{:S(2)}, u32[]{:S(2)}) %collective-permute-start.2) | collective-permute-done | bytes 32800 | tf_op jit(solution)/shard_map/ppermute | solution.py:356
  69.0 9.2 %all_to_all.15.x = f32[4,64,256]{2,1,0:T(8,128)S(1)} all-to-all(f32[4,64,256]{2,1,0:T(8,128)S(1)} %pad_maximum_fusion), channel_id=1, replica_groups={{0,1,2,3},{4,5,6,7},{8,9,10,11},{12,13,14,15},{16,17,18,19},{20,21,22,2..., dimensions={0} | all-to-all | bytes 524288 | tf_op jit(solution)/shard_map/all_to_all | solution.py:362
  78.2 0.7 shard_map.136
  (5 shorter events, 0.1 us)
Async XLA Ops:
  0.6 15.1 %copy-start = (f32[2,4,16,256]{3,2,1,0:T(8,128)S(1)}, f32[2,4,16,256]{3,2,1,0:T(8,128)}, u32[]{:S(2)}) copy-start(f32[2,4,16,256]{3,2,1,0:T(8,128)} %field.3) | copy-start | bytes 393220
  1.8 13.9 %collective-permute-start = (f32[14,16,256]{2,1,0:T(8,128)S(1)}, f32[14,16,256]{2,1,0:T(8,128)S(1)}, u32[]{:S(2)}, u32[]{:S(2)}) collective-permute-start(f32[14,16,256]{2,1,0:T(8,128)S(1)} %get-tuple-element.12), channel_id=1, source_target_pairs={{0,16},{16,32},{32,48},{48,64},{64,80},{80,96},{96,112},{112,128},... | collective-permute-start | bytes 688136 | tf_op jit(solution)/shard_map/ppermute | solution.py:337
  6.4 17.9 %all-to-all-start.1 = ((f32[32,1,128]{2,1,0:T(1,128)}), f32[32,1,128]{2,1,0:T(1,128)S(1)}, u32[]{:S(2)}, u32[]{:S(2)}) async-start(f32[32,1,128]{2,1,0:T(1,128)} %broadcast_in_dim.16), calls=%async_computation.1 | async-start | bytes 32768 | tf_op jit(solution)/shard_map/all_to_all | solution.py:339
  24.3 29.9 %all-to-all-start = ((f32[16,64,128]{2,1,0:T(8,128)}), f32[16,64,128]{2,1,0:T(8,128)S(1)}, u32[]{:S(2)}, u32[]{:S(2)}) async-start(f32[16,64,128]{2,1,0:T(8,128)} %shard_map.131), calls=%async_computation | async-start | bytes 1048576 | tf_op jit(solution)/shard_map/all_to_all | solution.py:342
  37.0 22.3 %copy-start.1 = (bf16[2,512,256]{2,1,0:T(8,128)(2,1)S(1)}, bf16[2,512,256]{2,1,0:T(8,128)(2,1)}, u32[]{:S(2)}) copy-start(bf16[2,512,256]{2,1,0:T(8,128)(2,1)} %constant.4.clone.tall) | copy-start | bytes 1572868
  57.4 6.2 %collective-permute-start.1 = (f32[2,8,512]{2,1,0:T(8,128)S(1)}, f32[2,8,512]{2,1,0:T(8,128)S(1)}, u32[]{:S(2)}, u32[]{:S(2)}) collective-permute-start(f32[2,8,512]{2,1,0:T(8,128)S(1)} %get-tuple-element.15.states), channel_id=1, source_target_pairs={{0,499},{1,0},{2,1},{3,2},{4,503},{5,4},{6,5},{7,6},{8,507},{9,8},... | collective-permute-start | bytes 98312 | tf_op jit(solution)/shard_map/ppermute | solution.py:349
  63.7 5.2 %collective-permute-start.2 = (f32[2,8,512]{2,1,0:T(8,128)S(1)}, f32[2,8,512]{2,1,0:T(8,128)S(1)}, u32[]{:S(2)}, u32[]{:S(2)}) collective-permute-start(f32[2,8,512]{2,1,0:T(8,128)S(1)} %shard_map.134.states), channel_id=1, source_target_pairs={{0,499},{1,0},{2,1},{3,2},{4,503},{5,4},{6,5},{7,6},{8,507},{9,8},... | collective-permute-start | bytes 98312 | tf_op jit(solution)/shard_map/ppermute | solution.py:356
where the time goes:
time: 79.3 us; the launch traced here: 79 us
  starting transfers between devices  29.9 us (38%)
  waiting for transfers between devices  25.9 us (33%)
  Pallas kernels  12.5 us (16%)
  blocking collectives  9.25 us (12%)
    all_to_all x1, waiting for transfers between devices, shards(): x = lax.all_to_all(packed, 'trans', 0, 0, tiled=True)  17.2 us
    all_to_all x1, starting transfers between devices, shards(): x = lax.all_to_all(packed, 'trans', 0, 0, tiled=True)  12.7 us
    pallas_call x7, Pallas kernels, call(): pl.pallas_call(body, out_shape=[kind(shape, bf16 if shape == TABLE else f...  12.5 us
    all_to_all x1, starting transfers between devices, shards(): charges = lax.all_to_all(charges, 'beam', 0, 0, tiled=True)  9.38 us
    all_to_all x1, blocking collectives, shards(): y = lax.all_to_all(both, 'trans', 0, 0, tiled=True, axis_index_groups=QUADS)  9.25 us
    all_to_all x1, waiting for transfers between devices, shards(): charges = lax.all_to_all(charges, 'beam', 0, 0, tiled=True)  7.69 us
    ppermute x1, starting transfers between devices, shards(): received = lax.ppermute(send, 'beam', NEXT_BEAM)  3.94 us
    ppermute x1, starting transfers between devices, shards(): home = lax.ppermute(final, JOINT, TO_PREVIOUS)  1.92 us
  transfers between devices with their start and end apart: 5, of which 3 were waited for; matrix products, arithmetic and copies ran while one was open for 1% of the time, Pallas kernels for 9%

commit v1 on v0

--- a/solution.py
+++ b/solution.py
@@ -259,15 +259,18 @@
     probe(fr, fi, take(2), take(3), re, im)
 
 
-def third_body(states, extra, re, im, out):
+def third_body(states, extra, re, im, out, lines):
     angles = states[0]
     energies = (
         states[1]
         - kick_gain * (re[...] * jnp.cos(angles) - im[...] * jnp.sin(angles))
         - extra[1, 0:1, 0:1]
     )
-    out[0] = angles + energies
-    out[1] = energies
+    for k, value in enumerate((angles + energies, energies)):
+        out[k] = value
+        for half in range(2):
+            at = (k * 2 + half) * 8
+            lines[at : at + 8, :] = value[:, half * 256 : half * 256 + 256]
 
 
 def fourth_body(field, states, own, received, extra, tall, out):
@@ -352,12 +355,13 @@
         [(2, GRID, GRID), line, line, TABLE],
         x, states, own, received, extra, tall, room=24,
     )
-    (final,) = call(third_body, [state_shape], following, extra, re, im, room=24)
-    home = lax.ppermute(final, JOINT, TO_PREVIOUS)
+    final, lines = call(
+        third_body, [state_shape, (32, 256)], following, extra, re, im, room=24
+    )
+    home = lax.ppermute(lines, JOINT, TO_PREVIOUS)
     (bands,) = call(
         fourth_body, [(4, 32, GRID)], field, final, own, received, extra, tall, room=24
     )
-    home = jnp.concatenate([home[..., :256], home[..., 256:]], axis=1).reshape(32, 256)
     both = jnp.concatenate([bands, jnp.broadcast_to(home[None], (4, 32, 256))], axis=1)
     y = lax.all_to_all(both, "trans", 0, 0, tiled=True, axis_index_groups=QUADS)
     return tuple(

time: 79.3 us -> 79.3 us (level)
  no operation moved by 1% of the time
where the time goes in v1:
time: 79.3 us; the launch traced here: 78.9 us
  starting transfers between devices  29.9 us (38%)
  waiting for transfers between devices  25.9 us (33%)
  Pallas kernels  12.5 us (16%)
  blocking collectives  9.23 us (12%)
    all_to_all x1, waiting for transfers between devices, shards(): x = lax.all_to_all(packed, 'trans', 0, 0, tiled=True)  17.2 us
    all_to_all x1, starting transfers between devices, shards(): x = lax.all_to_all(packed, 'trans', 0, 0, tiled=True)  12.7 us
    pallas_call x7, Pallas kernels, call(): pl.pallas_call(body, out_shape=[kind(shape, bf16 if shape == TABLE else f...  12.5 us
    all_to_all x1, starting transfers between devices, shards(): charges = lax.all_to_all(charges, 'beam', 0, 0, tiled=True)  9.38 us
    all_to_all x1, blocking collectives, shards(): y = lax.all_to_all(both, 'trans', 0, 0, tiled=True, axis_index_groups=QUADS)  9.23 us
    all_to_all x1, waiting for transfers between devices, shards(): charges = lax.all_to_all(charges, 'beam', 0, 0, tiled=True)  7.69 us
    ppermute x1, starting transfers between devices, shards(): received = lax.ppermute(send, 'beam', NEXT_BEAM)  3.94 us
    ppermute x1, starting transfers between devices, shards(): home = lax.ppermute(lines, JOINT, TO_PREVIOUS)  1.92 us
  transfers between devices with their start and end apart: 5, of which 3 were waited for; matrix products, arithmetic and copies ran while one was open for 1% of the time, Pallas kernels for 9%

profile of v1, /device:TPU:1, one launch (start us, length us, event | category | flops | bytes accessed | tf_op | source)
XLA Modules:
  0.0 78.9 jit_solution(2813795478003184541)
XLA Ops:
  0.6 0.0 copy-start
  0.6 1.2 %shard_map.130 = (f32[14,16,256]{2,1,0:T(8,128)S(1)}, f32[8,8,512]{2,1,0:T(8,128)S(1)}, f32[1,128]{1,0:T(1,128)S(1)}) custom-call(f32[2,4,16,256]{3,2,1,0:T(8,128)} %field.3, f32[4,4096]{1,0:T(4,128)} %phases.1, f32[4,4096]{1,0:T(4,128)} %energy.1, s32[4,4096]{1,0:T(4,128)} %row.1, s32[4,4096]{1,0:T(4,128)} %col.1, s32[4,4096]{1,0:T(4,128)} %weight.1, s32[4]{0:T(128)} %charge.1), custom_call_target="tpu_custom_call" | custom-call | tf_op jit(solution)/shard_map/pallas_call | solution.py:318
  1.8 3.9 %collective-permute-start = (f32[14,16,256]{2,1,0:T(8,128)S(1)}, f32[14,16,256]{2,1,0:T(8,128)S(1)}, u32[]{:S(2)}, u32[]{:S(2)}) collective-permute-start(f32[14,16,256]{2,1,0:T(8,128)S(1)} %get-tuple-element.14), channel_id=1, source_target_pairs={{0,16},{16,32},{32,48},{48,64},{64,80},{80,96},{96,112},{112,128},... | collective-permute-start | bytes 688136 | tf_op jit(solution)/shard_map/ppermute | solution.py:340
  5.8 0.6 broadcast_in_dim.7
  6.4 9.4 %all-to-all-start.1 = ((f32[32,1,128]{2,1,0:T(1,128)}), f32[32,1,128]{2,1,0:T(1,128)S(1)}, u32[]{:S(2)}, u32[]{:S(2)}) async-start(f32[32,1,128]{2,1,0:T(1,128)} %broadcast_in_dim.7), calls=%async_computation.1 | async-start | bytes 32768 | tf_op jit(solution)/shard_map/all_to_all | solution.py:342
  15.8 0.0 collective-permute-done.received
  15.8 0.0 copy-done
  15.8 0.8 %shard_map.131 = f32[16,64,128]{2,1,0:T(8,128)} custom-call(f32[2,4,16,256]{3,2,1,0:T(8,128)S(1)} %copy-done, f32[14,16,256]{2,1,0:T(8,128)S(1)} %collective-permute-done.received), custom_call_target="tpu_custom_call" | custom-call | tf_op jit(solution)/shard_map/pallas_call | solution.py:318
  16.6 7.7 %all-to-all-done.1 = f32[32,1,128]{2,1,0:T(1,128)S(1)} async-done(((f32[32,1,128]{2,1,0:T(1,128)}), f32[32,1,128]{2,1,0:T(1,128)S(1)}, u32[]{:S(2)}, u32[]{:S(2)}) %all-to-all-start.1) | async-done | bytes 16416 | tf_op jit(solution)/shard_map/all_to_all | solution.py:342
  24.3 12.7 %all-to-all-start = ((f32[16,64,128]{2,1,0:T(8,128)}), f32[16,64,128]{2,1,0:T(8,128)S(1)}, u32[]{:S(2)}, u32[]{:S(2)}) async-start(f32[16,64,128]{2,1,0:T(8,128)} %shard_map.131), calls=%async_computation | async-start | bytes 1048576 | tf_op jit(solution)/shard_map/all_to_all | solution.py:345
  37.0 0.0 copy-start.1
  37.0 17.2 %all-to-all-done.x = f32[16,64,128]{2,1,0:T(8,128)S(1)} async-done(((f32[16,64,128]{2,1,0:T(8,128)}), f32[16,64,128]{2,1,0:T(8,128)S(1)}, u32[]{:S(2)}, u32[]{:S(2)}) %all-to-all-start) | async-done | bytes 524320 | tf_op jit(solution)/shard_map/all_to_all | solution.py:345
  54.2 3.1 %shard_map.132 = (f32[2,8,512]{2,1,0:T(8,128)S(1)}, f32[4,8,128]{2,1,0:T(8,128)S(1)}, f32[8,512]{1,0:T(8,128)}, f32[8,512]{1,0:T(8,128)}) custom-call(f32[16,64,128]{2,1,0:T(8,128)S(1)} %all-to-all-done.x, f32[8,8,512]{2,1,0:T(8,128)S(1)} %get-tuple-element.15.own, f32[14,16,256]{2,1,0:T(8,128)S(1)} %collective-permute-done.received, f32[1,128]{1,0:T(1,128)S(1)} %bitcast.3, ...), custom_call_target="tpu_custom_call" | custom-call | tf_op jit(solution)/shard_map/pallas_call | solution.py:318
  57.4 1.9 %collective-permute-start.1 = (f32[2,8,512]{2,1,0:T(8,128)S(1)}, f32[2,8,512]{2,1,0:T(8,128)S(1)}, u32[]{:S(2)}, u32[]{:S(2)}) collective-permute-start(f32[2,8,512]{2,1,0:T(8,128)S(1)} %get-tuple-element.17.states), channel_id=1, source_target_pairs={{0,499},{1,0},{2,1},{3,2},{4,503},{5,4},{6,5},{7,6},{8,507},{9,8},... | collective-permute-start | bytes 98312 | tf_op jit(solution)/shard_map/ppermute | solution.py:352
  59.3 0.0 copy-done.1
  59.3 4.3 %shard_map.133 = (f32[2,256,256]{2,1,0:T(8,128)S(1)}, f32[8,512]{1,0:T(8,128)S(1)}, f32[8,512]{1,0:T(8,128)S(1)}, bf16[2,512,256]{2,1,0:T(8,128)(2,1)S(1)}) custom-call(f32[16,64,128]{2,1,0:T(8,128)S(1)} %all-to-all-done.x, f32[2,8,512]{2,1,0:T(8,128)S(1)} %get-tuple-element.17.states, f32[8,8,512]{2,1,0:T(8,128)S(1)} %get-tuple-element.15.own, ...), custom_call_target="tpu_custom_call" | custom-call | tf_op jit(solution)/shard_map/pallas_call | solution.py:318
  63.6 0.0 collective-permute-done.1.states
  63.6 0.1 shard_map.134
  63.7 1.9 %collective-permute-start.2 = (f32[32,256]{1,0:T(8,128)S(1)}, f32[32,256]{1,0:T(8,128)S(1)}, u32[]{:S(2)}, u32[]{:S(2)}) collective-permute-start(f32[32,256]{1,0:T(8,128)S(1)} %get-tuple-element.24), channel_id=1, source_target_pairs={{0,499},{1,0},{2,1},{3,2},{4,503},{5,4},{6,5},{7,6},{8,507},{9,8},... | collective-permute-start | bytes 98312 | tf_op jit(solution)/shard_map/ppermute | solution.py:361
  65.6 2.2 %shard_map.135 = f32[4,32,256]{2,1,0:T(8,128)S(1)} custom-call(f32[2,256,256]{2,1,0:T(8,128)S(1)} %get-tuple-element.19.field, f32[2,8,512]{2,1,0:T(8,128)S(1)} %get-tuple-element.22.states, f32[8,8,512]{2,1,0:T(8,128)S(1)} %get-tuple-element.15.own, f32[14,16,256]{2,1,0:T(8,128)S(1)} %collective-permute-done.received, ...), custom_call_target="tpu_custom_call" | custom-call | tf_op jit(solution)/shard_map/pallas_call | solution.py:318
  67.9 1.1 %collective-permute-done.2 = f32[32,256]{1,0:T(8,128)S(1)} collective-permute-done((f32[32,256]{1,0:T(8,128)S(1)}, f32[32,256]{1,0:T(8,128)S(1)}, u32[]{:S(2)}, u32[]{:S(2)}) %collective-permute-start.2) | collective-permute-done | bytes 32800 | tf_op jit(solution)/shard_map/ppermute | solution.py:361
  69.0 9.2 %all_to_all.15.x = f32[4,64,256]{2,1,0:T(8,128)S(1)} all-to-all(f32[4,64,256]{2,1,0:T(8,128)S(1)} %pad_maximum_fusion), channel_id=1, replica_groups={{0,1,2,3},{4,5,6,7},{8,9,10,11},{12,13,14,15},{16,17,18,19},{20,21,22,2..., dimensions={0} | all-to-all | bytes 524288 | tf_op jit(solution)/shard_map/all_to_all | solution.py:366
  78.2 0.7 shard_map.136
  (3 shorter events, 0.0 us)
Async XLA Ops:
  0.6 15.1 %copy-start = (f32[2,4,16,256]{3,2,1,0:T(8,128)S(1)}, f32[2,4,16,256]{3,2,1,0:T(8,128)}, u32[]{:S(2)}) copy-start(f32[2,4,16,256]{3,2,1,0:T(8,128)} %field.3) | copy-start | bytes 393220
  1.8 13.9 %collective-permute-start = (f32[14,16,256]{2,1,0:T(8,128)S(1)}, f32[14,16,256]{2,1,0:T(8,128)S(1)}, u32[]{:S(2)}, u32[]{:S(2)}) collective-permute-start(f32[14,16,256]{2,1,0:T(8,128)S(1)} %get-tuple-element.14), channel_id=1, source_target_pairs={{0,16},{16,32},{32,48},{48,64},{64,80},{80,96},{96,112},{112,128},... | collective-permute-start | bytes 688136 | tf_op jit(solution)/shard_map/ppermute | solution.py:340
  6.4 17.9 %all-to-all-start.1 = ((f32[32,1,128]{2,1,0:T(1,128)}), f32[32,1,128]{2,1,0:T(1,128)S(1)}, u32[]{:S(2)}, u32[]{:S(2)}) async-start(f32[32,1,128]{2,1,0:T(1,128)} %broadcast_in_dim.7), calls=%async_computation.1 | async-start | bytes 32768 | tf_op jit(solution)/shard_map/all_to_all | solution.py:342
  24.3 29.9 %all-to-all-start = ((f32[16,64,128]{2,1,0:T(8,128)}), f32[16,64,128]{2,1,0:T(8,128)S(1)}, u32[]{:S(2)}, u32[]{:S(2)}) async-start(f32[16,64,128]{2,1,0:T(8,128)} %shard_map.131), calls=%async_computation | async-start | bytes 1048576 | tf_op jit(solution)/shard_map/all_to_all | solution.py:345
  37.0 22.3 %copy-start.1 = (bf16[2,512,256]{2,1,0:T(8,128)(2,1)S(1)}, bf16[2,512,256]{2,1,0:T(8,128)(2,1)}, u32[]{:S(2)}) copy-start(bf16[2,512,256]{2,1,0:T(8,128)(2,1)} %constant.4.clone.tall) | copy-start | bytes 1572868
  57.4 6.2 %collective-permute-start.1 = (f32[2,8,512]{2,1,0:T(8,128)S(1)}, f32[2,8,512]{2,1,0:T(8,128)S(1)}, u32[]{:S(2)}, u32[]{:S(2)}) collective-permute-start(f32[2,8,512]{2,1,0:T(8,128)S(1)} %get-tuple-element.17.states), channel_id=1, source_target_pairs={{0,499},{1,0},{2,1},{3,2},{4,503},{5,4},{6,5},{7,6},{8,507},{9,8},... | collective-permute-start | bytes 98312 | tf_op jit(solution)/shard_map/ppermute | solution.py:352
  63.7 5.2 %collective-permute-start.2 = (f32[32,256]{1,0:T(8,128)S(1)}, f32[32,256]{1,0:T(8,128)S(1)}, u32[]{:S(2)}, u32[]{:S(2)}) collective-permute-start(f32[32,256]{1,0:T(8,128)S(1)} %get-tuple-element.24), channel_id=1, source_target_pairs={{0,499},{1,0},{2,1},{3,2},{4,503},{5,4},{6,5},{7,6},{8,507},{9,8},... | collective-permute-start | bytes 98312 | tf_op jit(solution)/shard_map/ppermute | solution.py:361
